TPU v7x, 128 devices: a whole 4x4x4 slice. The times are simulated.
128 devices in a mesh: row: 8 (over y, core), col: 16 (over x, z).
Axes of the slice: x: 4, y: 4, z: 4, core: 2. Of those that a mesh axis runs over, the one named last changes fastest.
Arguments:
- trail_rows: bfloat16 [24576, 8192], P('row', 'col'), may hold values from -0.0390625 to 0.0390625
- rows_first: bfloat16 [512, 8192], P(None, 'col'), may hold values from -0.25 to 0.25
- rows_second: bfloat16 [512, 8192], P(None, 'col'), may hold values from -0.25 to 0.25
- diag_first: float32 [512, 512], replicated, may hold values from -0.25 to 4, as said below
- diag_second: float32 [512, 512], replicated, may hold values from -0.25 to 4, as said below
- sub_block: float32 [512, 512], replicated, may hold values from -0.25 to 0.25
- cot_first: float32 [24576, 512], P('row', 'col'), may hold values from -6 to 6
- cot_second: float32 [24576, 512], P('row', 'col'), may hold values from -6 to 6
- cot_trail: float32 [24576, 8192], P('row', 'col'), may hold values from -6 to 6
- cot_rows_first: float32 [512, 8192], P('row', 'col'), may hold values from -6 to 6
- cot_rows_second: float32 [512, 8192], P('row', 'col'), may hold values from -6 to 6
Outputs:
- new_trail: float32 [24576, 8192], P('row', 'col')
- new_rows_first: float32 [512, 8192], P('row', 'col')
- new_rows_second: float32 [512, 8192], P('row', 'col')
- solved_first: float32 [24576, 512], P('row', 'col')
- solved_second: float32 [24576, 512], P('row', 'col')
Inputs may be any that keep to these rules, and one draw needn't show every extreme that they name: `diag_first`: lower triangular; the diagonal lies between 1 and 4, entries above it are zero. `diag_second`: lower triangular; the diagonal lies between 1 and 4, entries above it are zero.
All inputs are finite; a program needn't handle non-finite values.
Results may differ from a plain program's by a relative error of at most 0.0021.
Values sent between devices are 32-bit elements; how exact they have to be, the bound alone decides.
A program may use at most 128 MiB of HBM per device.

v0:
```python
import jax
import jax.numpy as jnp
from jax import lax
from jax.sharding import PartitionSpec as P


def solve_right(cotangent, factor):
    return lax.linalg.triangular_solve(factor, cotangent, left_side=False, lower=True)


def solve_panels(cot_first, cot_second, diag_first, diag_second, sub_block):
    solved_second = solve_right(cot_second, diag_second)
    carried = cot_first - jnp.dot(
        solved_second,
        sub_block,
        precision=lax.Precision.HIGHEST,
        preferred_element_type=jnp.float32,
    )
    solved_first = solve_right(carried, diag_first)
    return (solved_first, solved_second)


def transposed_product(left, right):
    return lax.dot_general(
        left, right, (((0,), (0,)), ((), ())), preferred_element_type=jnp.float32
    )


def on_device(
    trail_rows,
    rows_first,
    rows_second,
    diag_first,
    diag_second,
    sub_block,
    cot_first,
    cot_second,
    cot_trail,
    cot_rows_first,
    cot_rows_second,
):
    width = cot_first.shape[1]
    local_cols = trail_rows.shape[1]
    col_start = lax.axis_index("col") * width
    whole_first, whole_second = (
        lax.all_gather(cot_first, "col", axis=1, tiled=True),
        lax.all_gather(cot_second, "col", axis=1, tiled=True),
    )
    solved_first, solved_second = solve_panels(
        whole_first, whole_second, diag_first, diag_second, sub_block
    )
    low_first = solved_first.astype(jnp.bfloat16)
    low_second = solved_second.astype(jnp.bfloat16)
    update = jnp.dot(low_second, rows_second, preferred_element_type=jnp.float32) + jnp.dot(
        low_first, rows_first, preferred_element_type=jnp.float32
    )
    new_trail = cot_trail - update
    summed = lax.psum_scatter(
        jnp.concatenate(
            [transposed_product(low_first, trail_rows), transposed_product(low_second, trail_rows)],
            axis=1,
        ),
        "row",
        scatter_dimension=0,
        tiled=True,
    )
    out_first = lax.dynamic_slice_in_dim(solved_first, col_start, width, 1)
    out_second = lax.dynamic_slice_in_dim(solved_second, col_start, width, 1)
    new_rows_first = cot_rows_first - summed[:, :local_cols]
    new_rows_second = cot_rows_second - summed[:, local_cols:]
    return (new_trail, new_rows_first, new_rows_second, out_first, out_second)


def solution(mesh):
    return jax.shard_map(
        on_device,
        mesh=mesh,
        in_specs=(
            P("row", "col"),
            P(None, "col"),
            P(None, "col"),
            P(),
            P(),
            P(),
            P("row", "col"),
            P("row", "col"),
            P("row", "col"),
            P("row", "col"),
            P("row", "col"),
        ),
        out_specs=(
            P("row", "col"),
            P("row", "col"),
            P("row", "col"),
            P("row", "col"),
            P("row", "col"),
        ),
        check_vma=False,
    )
```

profile of v0, /device:TPU:0, one launch (start us, length us, event | category | flops | bytes accessed | tf_op | source)
XLA Modules:
  0.0 250.9 jit_solution(3787478144796487247)
XLA Ops:
  8.7 2.3 fusion.35
  11.1 11.6 %while.5 = (s32[]{:T(128)}, f32[512,512]{1,0:T(8,128)}, s32[4,2]{0,1:T(2,128)S(1)}, f32[4,128,128]{2,1,0:T(8,128)S(1)}, s32[]{:T(128)}) while((s32[]{:T(128)}, f32[512,512]{1,0:T(8,128)}, s32[4,2]{0,1:T(2,128)S(1)}, f32[4,128,128]{2,1,0:T(8,128)S(1)}, s32[]{:T(128)}) %tuple.46), condition=%wide.while_cond.clone, body=%wide.while_body.clone.sunk | while | flops 2 | bytes 131189 | solution.py:8
  23.4 40.1 %custom-call.5 = f32[4,128,128]{1,2,0:T(8,128)S(1)} custom-call(f32[4,128,128]{2,1,0:T(8,128)} %copy-done.23), custom_call_target="InvertDiagBlocksLowerTriangular" | custom-call | tf_op jit(solution)/shard_map/triangular_solve/custom-call.1 | solution.py:8
  63.5 2.3 fusion.36
  66.6 14.0 %while.4 = (s32[]{:T(128)}, f32[512,512]{1,0:T(8,128)}, s32[4,2]{0,1:T(2,128)S(1)}, f32[4,128,128]{2,1,0:T(8,128)}, s32[]{:T(128)}) while((s32[]{:T(128)}, f32[512,512]{1,0:T(8,128)}, s32[4,2]{0,1:T(2,128)S(1)}, f32[4,128,128]{2,1,0:T(8,128)}, s32[]{:T(128)}) %tuple.55), condition=%wide.while_cond, body=%wide.while_body.sunk | while | flops 2 | bytes 132205 | solution.py:8
  67.1 2.9 %bitcast_dynamic-update-slice_fusion.4 = f32[4,128,128]{2,1,0:T(8,128)} fusion(f32[4,128,128]{2,1,0:T(8,128)} %get-tuple-element.122, s32[]{:T(128)S(6)} %copy.34, f32[512,512]{1,0:T(8,128)} %get-tuple-element.125, s32[]{:T(128)} %bitcast.55, s32[]{:T(128)} %bitcast.56), kind=kLoop, calls=%fused_computation.clone.1 | loop fusion | bytes 132100 | tf_op jit(solution)/shard_map/triangular_solve | solution.py:8
  70.7 2.9 %bitcast_dynamic-update-slice_fusion.4 = f32[4,128,128]{2,1,0:T(8,128)} fusion(f32[4,128,128]{2,1,0:T(8,128)} %get-tuple-element.122, s32[]{:T(128)S(6)} %copy.34, f32[512,512]{1,0:T(8,128)} %get-tuple-element.125, s32[]{:T(128)} %bitcast.55, s32[]{:T(128)} %bitcast.56), kind=kLoop, calls=%fused_computation.clone.1 | loop fusion | bytes 132100 | tf_op jit(solution)/shard_map/triangular_solve | solution.py:8
  74.2 2.9 %bitcast_dynamic-update-slice_fusion.4 = f32[4,128,128]{2,1,0:T(8,128)} fusion(f32[4,128,128]{2,1,0:T(8,128)} %get-tuple-element.122, s32[]{:T(128)S(6)} %copy.34, f32[512,512]{1,0:T(8,128)} %get-tuple-element.125, s32[]{:T(128)} %bitcast.55, s32[]{:T(128)} %bitcast.56), kind=kLoop, calls=%fused_computation.clone.1 | loop fusion | bytes 132100 | tf_op jit(solution)/shard_map/triangular_solve | solution.py:8
  77.7 2.9 %bitcast_dynamic-update-slice_fusion.4 = f32[4,128,128]{2,1,0:T(8,128)} fusion(f32[4,128,128]{2,1,0:T(8,128)} %get-tuple-element.122, s32[]{:T(128)S(6)} %copy.34, f32[512,512]{1,0:T(8,128)} %get-tuple-element.125, s32[]{:T(128)} %bitcast.55, s32[]{:T(128)} %bitcast.56), kind=kLoop, calls=%fused_computation.clone.1 | loop fusion | bytes 132100 | tf_op jit(solution)/shard_map/triangular_solve | solution.py:8
  80.6 40.9 %custom-call.4 = f32[4,128,128]{1,2,0:T(8,128)} custom-call(f32[4,128,128]{2,1,0:T(8,128)} %get-tuple-element.20), custom_call_target="InvertDiagBlocksLowerTriangular" | custom-call | tf_op jit(solution)/shard_map/triangular_solve/custom-call.1 | solution.py:8
  121.5 3.0 %fusion.26 = f32[128,3072]{1,0:T(8,128)S(1)} fusion(f32[3072,512]{0,1:T(8,128)} %all-gather.3.cloned.1.call-done, f32[4,128,128]{1,2,0:T(8,128)} %custom-call.4), kind=kOutput, calls=%fused_computation.35 | convolution fusion | flops 603979776 | bytes 3211264 | tf_op jit(solution)/shard_map/triangular_solve/dot | solution.py:8
  124.5 3.6 %convolution_subtract_fusion.2 = f32[3072,128]{0,1:T(8,128)S(1)} fusion(f32[128,3072]{1,0:T(8,128)S(1)} %fusion.26, f32[3072,512]{0,1:T(8,128)} %all-gather.3.cloned.1.call-done, f32[512,512]{1,0:T(8,128)} %get-tuple-element.152), kind=kOutput, calls=%fused_computation.21 | convolution fusion | flops 604372992 | bytes 4784128 | tf_op jit(solution)/shard_map/triangular_solve/dot.8 | solution.py:8
  129.7 3.0 %convolution_subtract_fusion.4 = f32[3072,128]{0,1:T(8,128)S(1)} fusion(f32[3072,128]{0,1:T(8,128)S(1)} %bitcast.60, f32[3072,128]{0,1:T(8,128)S(1)} %fusion.47, f32[3072,512]{0,1:T(8,128)S(1)} %copy-done.19, f32[512,512]{1,0:T(8,128)} %get-tuple-element.152), kind=kOutput, calls=%fused_computation.23 | convolution fusion | flops 1209139200 | bytes 6422528 | tf_op jit(solution)/shard_map/triangular_solve/dot.10 | solution.py:8
  134.3 4.4 %fusion.15 = f32[3072,128]{0,1:T(8,128)S(1)} fusion(f32[3072,128]{0,1:T(8,128)S(1)} %bitcast.61, f32[3072,128]{0,1:T(8,128)S(1)} %fusion.47, f32[3072,128]{0,1:T(8,128)S(1)} %fusion.46, f32[3072,512]{0,1:T(8,128)S(1)} %copy-done.19, f32[512,512]{1,0:T(8,128)} %get-tuple-element.152), kind=kOutput, calls=%fused_computation.25 | convolution fusion | flops 1814691840 | bytes 8060928 | tf_op jit(solution)/shard_map/triangular_solve/dot.12 | solution.py:8
  141.7 4.4 %fusion.31 = f32[512,512]{0,1:T(8,128)} fusion(bf16[3072,512]{1,0:T(8,128)(2,1)S(1)} %copy-done, f32[3072,128]{0,1:T(8,128)S(1)} %bitcast.62, f32[3072,128]{0,1:T(8,128)S(1)} %fusion.47, f32[3072,128]{0,1:T(8,128)S(1)} %fusion.46, f32[3072,128]{0,1:T(8,128)S(1)} %fusion.45), kind=kOutput, calls=%fused_computation.40 | convolution fusion | flops 1623195648 | bytes 10485760 | tf_op jit(solution)/shard_map/dot_general | solution.py:24
  146.1 6.6 %copy.21 = f32[3072,512]{1,0:T(8,128)} copy(f32[3072,512]{0,1:T(8,128)} %all-gather.5.cloned.1.call-done) | data formatting | bytes 12582912 | tf_op jit(solution)/shard_map/all_gather | solution.py:46
  152.7 14.4 %convolution_subtract_fusion = f32[3072,512]{1,0:T(8,128)S(1)} fusion(f32[3072,512]{1,0:T(8,128)} %copy.21, f32[512,512]{1,0:T(8,128)} %param.18, f32[3072,128]{0,1:T(8,128)} %bitcast.63, f32[3072,128]{0,1:T(8,128)} %copy-done.7, f32[3072,128]{0,1:T(8,128)} %copy-done.11, f32[3072,128]{0,1:T(8,128)} %copy-done.15), kind=kOutput, calls=%fused_computation.7 | convolution fusion | flops 9669967872 | bytes 19922944 | tf_op jit(solution)/shard_map/dot_general | solution.py:13
  168.6 3.5 %convolution_subtract_fusion.1 = f32[3072,128]{1,0:T(8,128)S(1)} fusion(f32[128,3072]{1,0:T(8,128)S(1)} %fusion.24, f32[3072,512]{1,0:T(8,128)S(1)} %convolution_subtract_fusion, f32[512,512]{1,0:T(8,128)} %get-tuple-element.151), kind=kOutput, calls=%fused_computation.20 | convolution fusion | flops 604372992 | bytes 4784128 | tf_op jit(solution)/shard_map/triangular_solve/dot.8 | solution.py:8
  173.7 6.5 %convolution_subtract_fusion.3 = f32[3072,128]{1,0:T(8,128)S(1)} fusion(f32[3072,128]{0,1:T(8,128)S(1)} %bitcast.66, f32[3072,128]{0,1:T(8,128)S(1)} %fusion.43, f32[3072,512]{1,0:T(8,128)S(1)} %convolution_subtract_fusion, f32[512,512]{1,0:T(8,128)} %get-tuple-element.151), kind=kOutput, calls=%fused_computation.22 | convolution fusion | flops 1209139200 | bytes 6422528 | tf_op jit(solution)/shard_map/triangular_solve/dot.10 | solution.py:8
  181.9 9.3 %fusion.12 = f32[3072,128]{1,0:T(8,128)S(1)} fusion(f32[3072,128]{0,1:T(8,128)S(1)} %bitcast.67, f32[3072,128]{0,1:T(8,128)S(1)} %fusion.43, f32[3072,128]{0,1:T(8,128)S(1)} %fusion.42, f32[3072,512]{1,0:T(8,128)S(1)} %convolution_subtract_fusion, f32[512,512]{1,0:T(8,128)} %get-tuple-element.151), kind=kOutput, calls=%fused_computation.24 | convolution fusion | flops 1814691840 | bytes 8060928 | tf_op jit(solution)/shard_map/triangular_solve/dot.12 | solution.py:8
  198.7 2.8 %pad_maximum_fusion.1 = f32[3072,512]{0,1:T(8,128)S(1)} fusion(f32[3072,128]{0,1:T(8,128)S(1)} %bitcast.69, f32[3072,128]{0,1:T(8,128)} %copy-done.9, f32[3072,128]{0,1:T(8,128)} %copy-done.13, f32[3072,128]{0,1:T(8,128)} %copy-done.17), kind=kLoop, calls=%fused_computation.5 | loop fusion | flops 4718592 | bytes 12582912 | tf_op jit(solution)/shard_map/triangular_solve/concatenate.5 | solution.py:8
  204.9 4.3 %fusion.33 = f32[3072,512]{1,0:T(8,128)} fusion(bf16[512,512]{1,0:T(8,128)(2,1)S(1)} %copy-done.26, f32[3072,128]{0,1:T(8,128)S(1)} %bitcast.65, f32[3072,128]{0,1:T(8,128)S(1)} %copy-done.8, f32[3072,128]{0,1:T(8,128)S(1)} %copy-done.12, f32[3072,128]{0,1:T(8,128)S(1)} %copy-done.16), kind=kOutput, calls=%fused_computation.42 | convolution fusion | flops 1623195648 | bytes 13107200 | tf_op jit(solution)/shard_map/dot_general | solution.py:54
  210.8 6.1 %add_subtract_fusion = f32[3072,512]{1,0:T(8,128)} fusion(f32[3072,512]{1,0:T(8,128)S(1)} %bitcast.72, f32[3072,512]{1,0:T(8,128)} %fusion.33, bf16[512,512]{1,0:T(8,128)(2,1)S(1)} %copy-done.21, f32[3072,128]{0,1:T(8,128)S(1)} %bitcast.70, f32[3072,128]{0,1:T(8,128)S(1)} %copy-done.10, f32[3072,128]{0,1:T(8,128)S(1)} %copy-done.14, ...), kind=kOutput, calls=%fused_computation.6 | convolution fusion | flops 1626341376 | bytes 25690112 | tf_op jit(solution)/shard_map/dot_general | solution.py:54
  216.9 16.2 %reduce-scatter.4.cloned.1.call-done = f32[64,1024]{1,0:T(8,128)} async-done(((f32[512,1024]{1,0:T(8,128)}), f32[64,1024]{1,0:T(8,128)}) %reduce-scatter.4.cloned.1.call-update) | async-done | bytes 262160
  (112 shorter events, 51.0 us)
Async XLA Ops:
  7.2 134.5 %copy-start = (bf16[3072,512]{1,0:T(8,128)(2,1)S(1)}, bf16[3072,512]{1,0:T(8,128)(2,1)}, u32[]{:S(2)}) copy-start(bf16[3072,512]{1,0:T(8,128)(2,1)} %param.13) | copy-start | bytes 9437188
  7.2 114.3 %all-gather.3.cloned.1.call-start = ((), (), s32[]{:S(2)}) async-start(), calls=%async_computation.1 | async-start | bytes 6684672 | tf_op jit(solution)/shard_map/all_gather | solution.py:47
  7.9 138.2 %all-gather.5.cloned.1.call-start = ((), (), s32[]{:S(2)}) async-start(), calls=%async_computation.2 | async-start | bytes 6684672 | tf_op jit(solution)/shard_map/all_gather | solution.py:46
  8.7 224.4 %reduce-scatter.4.cloned.1.call-start = ((), (), s32[]{:S(2)}) async-start(), calls=%async_computation.3 | async-start | bytes 2359296
  121.5 6.6 %copy-start.22 = (f32[4,128,128]{1,2,0:T(8,128)S(1)}, f32[4,128,128]{1,2,0:T(8,128)}, u32[]{:S(2)}) copy-start(f32[4,128,128]{1,2,0:T(8,128)} %custom-call.4) | copy-start | bytes 786436
  124.5 16.0 %copy-start.2 = (f32[128,3072]{1,0:T(8,128)}, f32[128,3072]{1,0:T(8,128)S(1)}, u32[]{:S(2)}) copy-start(f32[128,3072]{1,0:T(8,128)S(1)} %fusion.26) | copy-start | bytes 4718596
  124.5 5.2 %copy-start.19 = (f32[3072,512]{0,1:T(8,128)S(1)}, f32[3072,512]{0,1:T(8,128)}, u32[]{:S(2)}) copy-start(f32[3072,512]{0,1:T(8,128)} %all-gather.3.cloned.1.call-done) | copy-start | bytes 18874372
  129.7 10.8 %copy-start.7 = (f32[3072,128]{0,1:T(8,128)}, f32[3072,128]{0,1:T(8,128)S(1)}, u32[]{:S(2)}) copy-start(f32[3072,128]{0,1:T(8,128)S(1)} %fusion.47) | copy-start | bytes 4718596
  134.3 6.2 %copy-start.11 = (f32[3072,128]{0,1:T(8,128)}, f32[3072,128]{0,1:T(8,128)S(1)}, u32[]{:S(2)}) copy-start(f32[3072,128]{0,1:T(8,128)S(1)} %fusion.46) | copy-start | bytes 4718596
  168.6 24.2 %copy-start.4 = (f32[128,3072]{1,0:T(8,128)}, f32[128,3072]{1,0:T(8,128)S(1)}, u32[]{:S(2)}) copy-start(f32[128,3072]{1,0:T(8,128)S(1)} %fusion.24) | copy-start | bytes 4718596
  173.7 19.1 %copy-start.9 = (f32[3072,128]{0,1:T(8,128)}, f32[3072,128]{0,1:T(8,128)S(1)}, u32[]{:S(2)}) copy-start(f32[3072,128]{0,1:T(8,128)S(1)} %fusion.43) | copy-start | bytes 4718596
  181.9 10.9 %copy-start.13 = (f32[3072,128]{0,1:T(8,128)}, f32[3072,128]{0,1:T(8,128)S(1)}, u32[]{:S(2)}) copy-start(f32[3072,128]{0,1:T(8,128)S(1)} %fusion.42) | copy-start | bytes 4718596
  198.7 2.8 %copy-start.3 = (f32[128,3072]{1,0:T(8,128)S(1)}, f32[128,3072]{1,0:T(8,128)}, u32[]{:S(2)}) copy-start(f32[128,3072]{1,0:T(8,128)} %copy-done.2) | copy-start | bytes 4718596
  198.7 3.3 %copy-start.8 = (f32[3072,128]{0,1:T(8,128)S(1)}, f32[3072,128]{0,1:T(8,128)}, u32[]{:S(2)}) copy-start(f32[3072,128]{0,1:T(8,128)} %copy-done.7) | copy-start | bytes 4718596
  198.7 3.8 %copy-start.12 = (f32[3072,128]{0,1:T(8,128)S(1)}, f32[3072,128]{0,1:T(8,128)}, u32[]{:S(2)}) copy-start(f32[3072,128]{0,1:T(8,128)} %copy-done.11) | copy-start | bytes 4718596
  198.7 4.2 %copy-start.16 = (f32[3072,128]{0,1:T(8,128)S(1)}, f32[3072,128]{0,1:T(8,128)}, u32[]{:S(2)}) copy-start(f32[3072,128]{0,1:T(8,128)} %copy-done.15) | copy-start | bytes 4718596
  202.9 6.2 %slice-start = ((s8[6291456]{0:T(1024)(128)(4,1)}), s8[4194304]{0:T(1024)(128)(4,1)S(1)}, s32[]{:S(2)}) async-start(s8[6291456]{0:T(1024)(128)(4,1)} %bitcast.71), calls=%async_computation.4 | async-start | bytes 8388608
  204.8 4.3 %copy-start.6 = (f32[128,3072]{1,0:T(8,128)S(1)}, f32[128,3072]{1,0:T(8,128)}, u32[]{:S(2)}) copy-start(f32[128,3072]{1,0:T(8,128)} %copy-done.4) | copy-start | bytes 4718596
  204.8 4.3 %copy-start.10 = (f32[3072,128]{0,1:T(8,128)S(1)}, f32[3072,128]{0,1:T(8,128)}, u32[]{:S(2)}) copy-start(f32[3072,128]{0,1:T(8,128)} %copy-done.9) | copy-start | bytes 4718596
  204.8 4.3 %copy-start.14 = (f32[3072,128]{0,1:T(8,128)S(1)}, f32[3072,128]{0,1:T(8,128)}, u32[]{:S(2)}) copy-start(f32[3072,128]{0,1:T(8,128)} %copy-done.13) | copy-start | bytes 4718596
  204.9 4.7 %copy-start.18 = (f32[3072,128]{0,1:T(8,128)S(1)}, f32[3072,128]{0,1:T(8,128)}, u32[]{:S(2)}) copy-start(f32[3072,128]{0,1:T(8,128)} %copy-done.17) | copy-start | bytes 4718596
  204.9 5.8 %slice-start.1 = ((s8[6291456]{0:T(1024)(128)(4,1)}), s8[2097152]{0:T(1024)(128)(4,1)S(1)}, s32[]{:S(2)}) async-start(s8[6291456]{0:T(1024)(128)(4,1)} %bitcast.71), calls=%async_computation.5 | async-start | bytes 4194304
  204.9 5.9 %copy-start.21 = (bf16[512,512]{1,0:T(8,128)(2,1)S(1)}, bf16[512,512]{1,0:T(8,128)(2,1)}, u32[]{:S(2)}) copy-start(bf16[512,512]{1,0:T(8,128)(2,1)} %param.14) | copy-start | bytes 1572868
  210.8 33.4 %copy-start.1 = (bf16[3072,512]{1,0:T(8,128)(2,1)S(1)}, bf16[3072,512]{1,0:T(8,128)(2,1)}, u32[]{:S(2)}) copy-start(bf16[3072,512]{1,0:T(8,128)(2,1)} %param.13) | copy-start | bytes 9437188
  (8 other events, 11.5 us)
Sparse Core Ops, SparseCore 0:
  10.2 64.1 all-gather.2
  76.6 61.7 all-gather.4
  196.9 36.0 reduce-scatter.3
where the time goes:
time: 256 us; the launch traced here: 251 us
  other arithmetic  93.1 us (36%)
  matrix products  75.5 us (29%)
  local copies, waits for them, and re-layouts  50.1 us (20%)
  waiting for transfers between devices  17.6 us (7%)
  between operations  14.4 us (6%)
    another operation x7, other arithmetic, solve_right(): lax.linalg.triangular_solve(factor, cotangent, left_side=False, lower=True)  89.5 us
    another operation x14, matrix products, solve_right(): lax.linalg.triangular_solve(factor, cotangent, left_side=False, lower=True)  44.5 us
    another operation x26, local copies, waits for them, and re-layouts, solve_right(): lax.linalg.triangular_solve(factor, cotangent, left_side=False, lower=True)  26.2 us
    unnamed x4, waiting for transfers between devices  17.6 us
    unnamed x65, local copies, waits for them, and re-layouts  14.7 us
    dot_general x1, matrix products, solve_panels(): jnp.dot(solved_second, sub_block, precision=lax.Precision.HIGHEST, prefer...  14.4 us
    all_gather x1, local copies, waits for them, and re-layouts, on_device(): lax.all_gather(cot_first, 'col', axis=1, tiled=True)  6.56 us
    dot_general x2, matrix products, transposed_product(): lax.dot_general(left, right, (((0,), (0,)), ((), ())), preferred_element_...  6.3 us
  transfers between devices with their start and end apart: 3, of which 1 were waited for; matrix products, arithmetic and copies ran while one was open for 60% of the time, Pallas kernels for 0%

commit v1 on v0

v1 whole, which is shorter than its diff:
```python
import functools

import jax
import jax.numpy as jnp
from jax import lax
from jax.experimental import pallas as pl
from jax.experimental.pallas import tpu as pltpu
from jax.sharding import PartitionSpec as P

MESH = pl.DeviceIdType.MESH
BF = jnp.bfloat16
F32 = jnp.float32
W = 512
OFF = 2
NB = 512
HALF = NB // 2


def split(value):
    high = value.astype(BF)
    return high, (value - high.astype(F32)).astype(BF)


def dot(left, right):
    return jnp.dot(left, right, preferred_element_type=F32)


def dot3(left, right):
    lh, ll = left
    rh, rl = right
    return dot(lh, rh) + (dot(lh, rl) + dot(ll, rh))


def dot_tall(stacked, right):
    rh, rl = right
    rows = stacked.shape[0] // 2
    both = dot(stacked, rh)
    return both[:rows] + (both[rows:] + dot(stacked[:rows], rl))


def invert_lower(block):
    base, groups = 32, 4
    row = lax.broadcasted_iota(jnp.int32, (base, 128), 0)
    lane = lax.broadcasted_iota(jnp.int32, (base, 128), 1)
    group = lane // base
    first = group * base
    halves = []
    packs = []
    for half in range(2):
        part = block[128 * half : 128 * half + 128, 128 * half : 128 * half + 128]
        pack = jnp.zeros((base, 128), F32)
        for q in range(groups):
            pack = jnp.where(group == q, part[base * q : base * q + base], pack)
        packs.append(pack)
    pack = jnp.concatenate(packs, axis=0)
    row2, lane2, first2 = (jnp.concatenate([v, v], axis=0) for v in (row, lane, first))
    on_diag = row2 == lane2 - first2
    diag_cols = jnp.where(on_diag, pack, 0.0)
    diag_rows = jnp.take_along_axis(pack, first2 + row2, axis=1)
    unit = jnp.where(lane2 - first2 < row2, pack / diag_rows, 0.0)
    inv = jnp.where(on_diag, 1.0, 0.0).astype(F32)
    for k in range(base - 1):
        column = jnp.take_along_axis(unit, first2 + k, axis=1)
        pivot = jnp.concatenate(
            [jnp.broadcast_to(inv[k + base * h : k + base * h + 1], (base, 128)) for h in range(2)], axis=0
        )
        inv = inv - column * pivot
    pieces = []
    for half in range(2):
        mine = slice(base * half, base * half + base)
        scale = jnp.sum(diag_cols[mine], axis=0, keepdims=True)
        scaled = inv[mine] / scale
        full = jnp.concatenate([jnp.where(group == q, scaled, 0.0) for q in range(groups)], axis=0)
        zero = jnp.zeros((128, 128), F32)
        pieces.append(jnp.concatenate([full, zero] if half == 0 else [zero, full], axis=1))
    result = jnp.concatenate(pieces, axis=0)
    brow = lax.broadcasted_iota(jnp.int32, (HALF, HALF), 0)
    bcol = lax.broadcasted_iota(jnp.int32, (HALF, HALF), 1)
    for size in (32, 64, 128):
        below = (brow // size == bcol // size + 1) & (lax.rem(bcol // size, 2) == 0)
        low = jnp.where(below, block, 0.0)
        parts = split(result)
        result = result - dot3(parts, split(dot3(split(low), parts)))
    return result


def kernel(
    cs_ref, cf_ref, trail_ref, rs_ref, rf_ref, ds_ref, df_ref, e_ref, ct_ref, crf_ref, crs_ref,
    nt_ref, nrf_ref, nrs_ref, sf_ref, ss_ref,
    G, T, L, CT, TR, R, D, E, acc, XB, PB, HB, FB, CR, XS, inv_s, off_s, e_s,
    lsem, isem, osem, ssem, rsem, rs_send, rs_recv,
):
    K = G.shape[0] // 2
    N = 2 * K
    c = lax.axis_index("col")
    r = lax.axis_index("row")
    x, z = c // 4, lax.rem(c, 4)
    y, core = r // 2, lax.rem(r, 2)
    x_p, x_m = lax.rem(x + 1, 4), lax.rem(x + 3, 4)
    z_p, z_m = lax.rem(z + 1, 4), lax.rem(z + 3, 4)
    y_p, y_m = lax.rem(y + 1, 4), lax.rem(y + 3, 4)
    to = (
        ({"col": x_p * 4 + z, "row": r}, {"col": x_m * 4 + z, "row": r}),
        ({"col": x * 4 + z_p, "row": r}, {"col": x * 4 + z_m, "row": r}),
        ({"col": c, "row": 2 * y_p + core}, {"col": c, "row": 2 * y_m + core}),
    )
    other = {"col": c, "row": 2 * y + 1 - core}

    def own(g, source):
        k = lax.rem(g, K)
        lanes = pl.ds(pl.multiple_of(k * W, 128), W)
        return pltpu.make_async_copy(source.at[:, lanes], G.at[g, x, z], lsem.at[g])

    @pl.loop(0, K)
    def _(k):
        own(k, cs_ref).start()

    @pl.loop(0, K)
    def _(k):
        own(k + K, cf_ref).start()

    loads = [
        pltpu.make_async_copy(ds_ref, D.at[0], isem.at[0]),
        pltpu.make_async_copy(df_ref, D.at[1], isem.at[1]),
        pltpu.make_async_copy(e_ref, E, isem.at[2]),
        pltpu.make_async_copy(trail_ref, TR, isem.at[3]),
        pltpu.make_async_copy(rs_ref, R.at[:NB], isem.at[4]),
        pltpu.make_async_copy(rf_ref, R.at[NB:], isem.at[5]),
        pltpu.make_async_copy(crs_ref, CR.at[0], isem.at[6]),
        pltpu.make_async_copy(crf_ref, CR.at[1], isem.at[7]),
        pltpu.make_async_copy(ct_ref, CT, isem.at[8]),
    ]
    for load in loads:
        load.start()

    barrier = pltpu.get_barrier_semaphore()
    for pair in to:
        for device in pair:
            pl.semaphore_signal(barrier, 1, device_id=device, device_id_type=MESH)
    pl.semaphore_signal(barrier, 1, device_id=other, device_id_type=MESH)
    pl.semaphore_wait(barrier, 7)

    def hop(g, t, s, d, landing):
        i1, m1, p1 = ((x, x_m, x_p), (z, z_m, z_p))[t]
        i2, m2, p2 = ((z, z_m, z_p), (x, x_m, x_p))[t]
        near = lambda mine, minus, plus: (minus if d == 0 else plus)
        opposite = lambda mine: lax.rem(mine + 2, 4)
        rows, half = pl.ds(16 * t, 16), pl.ds(16 * t + 8 * d, 8)
        every = slice(None)
        if s == 0:
            a, b, part = (near(i1, m1, p1) if landing else i1), i2, rows
        elif s == 1:
            a, b, part = (opposite(i1) if landing else near(i1, m1, p1)), i2, half
        elif s == 2:
            a, b, part = every, (near(i2, m2, p2) if landing else i2), rows
        else:
            a, b, part = every, (opposite(i2) if landing else near(i2, m2, p2)), half
        ref = G.at[g, a, b, part] if t == 0 else G.at[g, b, a, part]
        axis = t if s < 2 else 1 - t
        index = t * 8 + s * 2 + d
        return pltpu.make_async_remote_copy(
            ref, ref, ssem.at[g, index], rsem.at[g, index], device_id=to[axis][d], device_id_type=MESH
        )

    def stage(g, s):
        if s == 0:
            own(g, cs_ref).wait()
        else:
            for t in range(2):
                for d in range(2):
                    hop(g, t, s - 1, d, True).wait_recv()
        if s < 4:
            for t in range(2):
                for d in range(2):
                    hop(g, t, s, d, False).start()

    def communicate(tick):
        for s in (3, 2, 1, 0, 4):
            g = tick - s * OFF
            if isinstance(tick, int):
                if 0 <= g < N:
                    stage(g, s)
            else:

                @pl.when((g >= 0) & (g < N))
                def _():
                    stage(g, s)

    communicate(0)
    loads[0].wait()
    loads[1].wait()
    communicate(1)

    @pl.loop(0, 4)
    def _(j):
        communicate(2 + j)
        panel, at = j // 2, pl.multiple_of(lax.rem(j, 2) * HALF, HALF)
        inverse = invert_lower(D[panel, pl.ds(at, HALF), pl.ds(at, HALF)])
        high, low = split(inverse.T)
        inv_s[j, :HALF] = high
        inv_s[j, HALF:] = low

    loads[2].wait()
    for panel in range(2):
        high, low = split(D[panel, HALF:, :HALF].T)
        off_s[panel, :HALF] = high
        off_s[panel, HALF:] = low
    high, low = split(E[...].T)
    e_s[:NB] = high
    e_s[NB:] = low
    acc[...] = jnp.zeros_like(acc)
    for load in loads[3:]:
        load.wait()
    for tick in range(6, 4 * OFF):
        communicate(tick)

    def solve(right, panel):
        x1 = dot_tall(inv_s[2 * panel + 1], split(right[HALF:]))
        x1_parts = split(x1)
        left = right[:HALF] - dot_tall(off_s[panel], x1_parts)
        x0 = dot_tall(inv_s[2 * panel], split(left))
        return x0, x1, split(x0), x1_parts

    def put(k, panel, solved, out_ref):
        x0, x1, (h0, _), (h1, _) = solved
        XS[:HALF] = x0
        XS[HALF:] = x1
        lanes = pl.ds(pl.multiple_of(k * W, 128), W)
        out_ref[:, lanes] = XS[pl.ds(pl.multiple_of(c * 32, 32), 32)]
        L[k, NB * panel : NB * panel + HALF] = h0
        L[k, NB * panel + HALF : NB * panel + NB] = h1
        rows = TR[pl.ds(pl.multiple_of(k * W, 128), W)]
        for q in range(2):
            part = slice(HALF * q, HALF * q + HALF)
            acc[panel, part] += dot((h0, h1)[q], rows)

    def reduce_copies(panel, s):
        base = panel * 5
        make = pltpu.make_async_remote_copy

        def remote(src, dst, i, device):
            return make(src, dst, rs_send.at[base + i], rs_recv.at[base + i], device_id=device, device_id_type=MESH)

        if s == 0:
            return [remote(PB.at[panel, 1], XB.at[panel], 0, other)]
        far = lax.rem(y + 2, 4)
        if s == 1:
            return [
                remote(PB.at[panel, 0, far, :32], HB.at[panel, 0], 1, to[2][0]),
                remote(PB.at[panel, 0, far, 32:], HB.at[panel, 1], 2, to[2][1]),
            ]
        return [
            remote(PB.at[panel, 0, y_p], FB.at[panel, 0], 3, to[2][0]),
            remote(PB.at[panel, 0, y_m], FB.at[panel, 1], 4, to[2][1]),
        ]

    def reduce_step(panel, s, out_ref):
        if s == 0:
            for q in range(4):
                PB[panel, 0, q] = acc[panel, pl.ds(pl.multiple_of(128 * q + 64 * core, 64), 64)]
                PB[panel, 1, q] = acc[panel, pl.ds(pl.multiple_of(128 * q + 64 * (1 - core), 64), 64)]
        elif s == 1:
            for copy in reduce_copies(panel, 0):
                copy.wait_recv()
            PB[panel, 0] += XB[panel]
        elif s == 2:
            for copy in reduce_copies(panel, 1):
                copy.wait_recv()
            PB[panel, 0, y_p, :32] += HB[panel, 0]
            PB[panel, 0, y_m, 32:] += HB[panel, 1]
        else:
            for copy in reduce_copies(panel, 2):
                copy.wait_recv()
            out_ref[...] = CR[panel] - ((PB[panel, 0, y] + FB[panel, 0]) + FB[panel, 1])
        if s < 3:
            for copy in reduce_copies(panel, s):
                copy.start()

    def store(k):
        rows = pl.ds(pl.multiple_of(k * W, W), W)
        return pltpu.make_async_copy(CT.at[rows], nt_ref.at[rows], osem.at[k])

    def trail(k):
        rows = pl.ds(pl.multiple_of(k * W, W), W)
        update = lax.dot_general(L[k], R[...], (((0,), (0,)), ((), ())), preferred_element_type=F32)
        CT[rows] -= update
        store(k).start()

    @pl.loop(0, K)
    def _(k):
        communicate(4 * OFF + k)
        solved = solve(G[k].reshape(NB, W), 0)
        put(k, 0, solved, ss_ref)
        T[k] = dot_tall(e_s[...], tuple(jnp.concatenate(p, axis=0) for p in zip(solved[2], solved[3])))

    @pl.loop(0, K)
    def _(k):
        communicate(4 * OFF + K + k)
        for s in range(4):

            @pl.when(k == s)
            def _():
                reduce_step(0, s, nrs_ref)

        put(k, 1, solve(G[K + k].reshape(NB, W) - T[k], 1), sf_ref)

        @pl.when(k >= 1)
        def _():
            trail(k - 1)

    reduce_step(1, 0, nrf_ref)
    trail(K - 1)
    reduce_step(1, 1, nrf_ref)

    @pl.loop(0, N)
    def _(g):
        for s in range(4):
            for t in range(2):
                for d in range(2):
                    hop(g, t, s, d, False).wait_send()

    reduce_step(1, 2, nrf_ref)

    @pl.loop(0, K)
    def _(k):
        store(k).wait()

    reduce_step(1, 3, nrf_ref)
    for panel in range(2):
        for s in range(3):
            for copy in reduce_copies(panel, s):
                copy.wait_send()


def on_device(
    trail_rows, rows_first, rows_second, diag_first, diag_second, sub_block,
    cot_first, cot_second, cot_trail, cot_rows_first, cot_rows_second,
):
    rows, cols = trail_rows.shape
    K = rows // W
    shape = jax.ShapeDtypeStruct
    hbm = pl.BlockSpec(memory_space=pl.ANY)
    vmem = pl.BlockSpec(memory_space=pltpu.VMEM)
    dma = pltpu.SemaphoreType.DMA
    new_trail, new_first, new_second, first_t, second_t = pl.pallas_call(
        kernel,
        out_shape=(
            shape((rows, cols), F32),
            shape((64, cols), F32),
            shape((64, cols), F32),
            shape((32, rows), F32),
            shape((32, rows), F32),
        ),
        in_specs=[hbm] * 11,
        out_specs=(hbm, vmem, vmem, vmem, vmem),
        scratch_shapes=[
            pltpu.VMEM((2 * K, 4, 4, 32, W), F32),
            pltpu.VMEM((K, NB, W), F32),
            pltpu.VMEM((K, 2 * NB, W), BF),
            pltpu.VMEM((rows, cols), F32),
            pltpu.VMEM((rows, cols), BF),
            pltpu.VMEM((2 * NB, cols), BF),
            pltpu.VMEM((2, NB, NB), F32),
            pltpu.VMEM((NB, NB), F32),
            pltpu.VMEM((2, NB, cols), F32),
            pltpu.VMEM((2, 4, 64, cols), F32),
            pltpu.VMEM((2, 2, 4, 64, cols), F32),
            pltpu.VMEM((2, 2, 32, cols), F32),
            pltpu.VMEM((2, 2, 64, cols), F32),
            pltpu.VMEM((2, 64, cols), F32),
            pltpu.VMEM((NB, W), F32),
            pltpu.VMEM((4, NB, HALF), BF),
            pltpu.VMEM((2, NB, HALF), BF),
            pltpu.VMEM((2 * NB, NB), BF),
            dma((2 * K,)),
            dma((9,)),
            dma((K,)),
            dma((2 * K, 16)),
            dma((2 * K, 16)),
            dma((10,)),
            dma((10,)),
        ],
        compiler_params=pltpu.CompilerParams(
            collective_id=0, has_side_effects=True, vmem_limit_bytes=62 * 1024 * 1024
        ),
    )(
        cot_second.T, cot_first.T, trail_rows, rows_second, rows_first, diag_second, diag_first,
        sub_block, cot_trail, cot_rows_first, cot_rows_second,
    )
    return new_trail, new_first, new_second, first_t.T, second_t.T


def solution(mesh):
    both = P("row", "col")
    col = P(None, "col")
    return jax.shard_map(
        on_device,
        mesh=mesh,
        in_specs=(both, col, col, P(), P(), P(), both, both, both, both, both),
        out_specs=(both,) * 5,
        check_vma=False,
    )
```

time: 256 us -> 109 us (0.43); the launches traced: 251 us -> 108 us
  Pallas kernels: 0 us -> 98 us
  other arithmetic: 93.1 us -> 0 us
  matrix products: 75.5 us -> 0 us
  local copies, waits for them, and re-layouts: 50.1 us -> 9.1 us
  waiting for transfers between devices: 17.6 us -> 0 us
  between operations: 14.4 us -> 0.68 us
    pallas_call x0 -> x1, Pallas kernels: none -> 98 us  [on_device(): pl.pallas_call(kernel, out_shape=(shape((rows, cols), F32), shape((64, co...]
    another operation x7 -> x0, other arithmetic: 89.5 us -> none  [solve_right(): lax.linalg.triangular_solve(factor, cotangent, left_side=False, lower=True)]
    another operation x14 -> x0, matrix products: 44.5 us -> none  [solve_right(): lax.linalg.triangular_solve(factor, cotangent, left_side=False, lower=True)]
    dot_general x5 -> x0, matrix products: 31 us -> none  [the longest x1 14.4 us: solve_panels(): jnp.dot(solved_second, sub_block, precision=lax.Precision.HIGHEST, prefer...]
    another operation x26 -> x0, local copies, waits for them, and re-layouts: 26.2 us -> none  [solve_right(): lax.linalg.triangular_solve(factor, cotangent, left_side=False, lower=True)]
    unnamed x4 -> x0, waiting for transfers between devices: 17.6 us -> none
    all_gather x1 -> x0, local copies, waits for them, and re-layouts: 6.56 us -> none  [on_device(): lax.all_gather(cot_first, 'col', axis=1, tiled=True)]
    unnamed x65 -> x13, local copies, waits for them, and re-layouts: 14.7 us -> 9.1 us
  transfers between devices with their start and end apart: 3 -> 0, of which waited for: 1 -> 0; matrix products, arithmetic and copies ran while one was open for 60% -> 0% of each run, Pallas kernels for 0% -> 0%
where the time goes in v1:
time: 109 us; the launch traced here: 108 us
  Pallas kernels  98 us (90%)
  local copies, waits for them, and re-layouts  9.1 us (8%)
    pallas_call x1, Pallas kernels, on_device(): pl.pallas_call(kernel, out_shape=(shape((rows, cols), F32), shape((64, co...  98 us
    unnamed x13, local copies, waits for them, and re-layouts  9.1 us

profile of v1, /device:TPU:0, one launch (start us, length us, event | category | flops | bytes accessed | tf_op | source)
XLA Modules:
  0.0 107.8 jit_solution(12636794684337020016)
XLA Ops:
  0.6 98.0 %shard_map.146 = (f32[3072,512]{1,0:T(8,128)}, f32[64,512]{1,0:T(8,128)}, f32[64,512]{1,0:T(8,128)}, f32[32,3072]{1,0:T(8,128)}, f32[32,3072]{1,0:T(8,128)}) custom-call(f32[32,3072]{1,0:T(8,128)} %bitcast.6, f32[32,3072]{1,0:T(8,128)} %bitcast.7, bf16[3072,512]{1,0:T(8,128)(2,1)} %trail_ref.1, bf16[512,512]{1,0:T(8,128)(2,1)} %rs_ref.1, ...), custom_call_target="tpu_custom_call" | custom-call | tf_op jit(solution)/shard_map/pallas_call | solution.py:345
  98.7 0.0 copy-start.3
  98.7 0.0 copy-start.2
  98.7 0.0 copy-start.1
  98.7 0.0 copy-start
  98.7 6.3 %copy.21 = f32[3072,512]{1,0:T(8,128)} copy(f32[3072,512]{1,0:T(8,128)} %get-tuple-element.20) | data formatting | bytes 12582912
  105.0 0.0 copy-done.3
  105.0 0.7 copy.22
  105.6 0.0 copy-done.2
  105.6 0.7 copy.23
  106.3 0.0 copy-done.1
  106.3 0.7 copy.24
  107.0 0.0 copy-done
  107.0 0.7 copy.25
Async XLA Ops:
  98.7 6.3 %copy-start.3 = (f32[64,512]{1,0:T(8,128)S(1)}, f32[64,512]{1,0:T(8,128)}, u32[]{:S(2)}) copy-start(f32[64,512]{1,0:T(8,128)} %get-tuple-element.21) | copy-start | bytes 393220
  98.7 7.0 %copy-start.2 = (f32[64,512]{1,0:T(8,128)S(1)}, f32[64,512]{1,0:T(8,128)}, u32[]{:S(2)}) copy-start(f32[64,512]{1,0:T(8,128)} %get-tuple-element.22) | copy-start | bytes 393220
  98.7 7.6 %copy-start.1 = (f32[32,3072]{1,0:T(8,128)S(1)}, f32[32,3072]{1,0:T(8,128)}, u32[]{:S(2)}) copy-start(f32[32,3072]{1,0:T(8,128)} %get-tuple-element.13) | copy-start | bytes 1179652
  98.7 8.4 %copy-start = (f32[32,3072]{1,0:T(8,128)S(1)}, f32[32,3072]{1,0:T(8,128)}, u32[]{:S(2)}) copy-start(f32[32,3072]{1,0:T(8,128)} %get-tuple-element.14) | copy-start | bytes 1179652

commit v2 on v1

v2 whole, which is shorter than its diff:
```python
import functools

import jax
import jax.numpy as jnp
from jax import lax
from jax.experimental import pallas as pl
from jax.experimental.pallas import tpu as pltpu
from jax.sharding import PartitionSpec as P

MESH = pl.DeviceIdType.MESH
BF = jnp.bfloat16
F32 = jnp.float32
W = 512
LEAD = (8, 6, 3, 1, 0)
FILL = (
    ((0, 0), (1, 0), (2, 0), (3, 0)),
    ((0, 1), (1, 1), (4, 0), (5, 0)),
    ((0, 2), (2, 1), (3, 1), (6, 0)),
    ((1, 2), (4, 1), (7, 0)),
    ((0, 3), (2, 2), (5, 1)),
)
NB = 512
HALF = NB // 2


def split(value):
    high = value.astype(BF)
    return high, (value - high.astype(F32)).astype(BF)


def dot(left, right):
    return jnp.dot(left, right, preferred_element_type=F32)


def dot3(left, right):
    lh, ll = left
    rh, rl = right
    return dot(lh, rh) + (dot(lh, rl) + dot(ll, rh))


def dot_tall(stacked, right):
    rh, rl = right
    rows = stacked.shape[0] // 2
    both = dot(stacked, rh)
    return both[:rows] + (both[rows:] + dot(stacked[:rows], rl))


def invert_lower(blocks):
    base, groups = 32, 4
    parts = 2 * len(blocks)
    shape = (base * parts, 128)
    row = lax.rem(lax.broadcasted_iota(jnp.int32, shape, 0), base)
    lane = lax.broadcasted_iota(jnp.int32, shape, 1)
    first = lane // base * base
    group = lane[:base] // base
    packs = []
    for block in blocks:
        for h in range(2):
            part = block[128 * h : 128 * h + 128, 128 * h : 128 * h + 128]
            pack = part[:base]
            for q in range(1, groups):
                pack = jnp.where(group == q, part[base * q : base * q + base], pack)
            packs.append(pack)
    pack = jnp.concatenate(packs, axis=0)
    on_diag = row == lane - first
    diag_cols = jnp.where(on_diag, pack, 0.0)
    diag_rows = jnp.take_along_axis(pack, first + row, axis=1)
    unit = jnp.where(lane - first < row, pack / diag_rows, 0.0)
    inv = jnp.where(on_diag, 1.0, 0.0).astype(F32)
    for k in range(base - 1):
        column = jnp.take_along_axis(unit, first + k, axis=1)
        pivot = jnp.concatenate(
            [jnp.broadcast_to(inv[k + base * h : k + base * h + 1], (base, 128)) for h in range(parts)], axis=0
        )
        inv = inv - column * pivot
    results = []
    zero = jnp.zeros((128, 128), F32)
    for i in range(len(blocks)):
        pieces = []
        for h in range(2):
            mine = slice(base * (2 * i + h), base * (2 * i + h) + base)
            scaled = inv[mine] / jnp.sum(diag_cols[mine], axis=0, keepdims=True)
            full = jnp.concatenate([jnp.where(group == q, scaled, 0.0) for q in range(groups)], axis=0)
            pieces.append(jnp.concatenate([full, zero] if h == 0 else [zero, full], axis=1))
        results.append(jnp.concatenate(pieces, axis=0))
    brow = lax.broadcasted_iota(jnp.int32, (HALF, HALF), 0)
    bcol = lax.broadcasted_iota(jnp.int32, (HALF, HALF), 1)
    for size in (32, 64, 128):
        below = (brow // size == bcol // size + 1) & (lax.rem(bcol // size, 2) == 0)
        halves = [split(result) for result in results]
        inner = [dot3(split(jnp.where(below, b, 0.0)), h) for b, h in zip(blocks, halves)]
        outer = [dot3(h, split(v)) for h, v in zip(halves, inner)]
        results = [result - v for result, v in zip(results, outer)]
    return results


def kernel(
    cs_ref, cf_ref, trail_ref, rs_ref, rf_ref, ds_ref, df_ref, e_ref, ct_ref, crf_ref, crs_ref,
    CT, nrf_ref, nrs_ref, sf_ref, ss_ref,
    G, T, L, TR, R, D, E, acc, XB, PB, HB, FB, CR, inv_s, off_s, e_s,
    lsem, isem, ssem, rsem, rs_send, rs_recv,
):
    K = G.shape[0] // 2
    N = 2 * K
    c = lax.axis_index("col")
    r = lax.axis_index("row")
    x, z = c // 4, lax.rem(c, 4)
    y, core = r // 2, lax.rem(r, 2)
    x_p, x_m = lax.rem(x + 1, 4), lax.rem(x + 3, 4)
    z_p, z_m = lax.rem(z + 1, 4), lax.rem(z + 3, 4)
    y_p, y_m = lax.rem(y + 1, 4), lax.rem(y + 3, 4)
    to = (
        ({"col": x_p * 4 + z, "row": r}, {"col": x_m * 4 + z, "row": r}),
        ({"col": x * 4 + z_p, "row": r}, {"col": x * 4 + z_m, "row": r}),
        ({"col": c, "row": 2 * y_p + core}, {"col": c, "row": 2 * y_m + core}),
    )
    other = {"col": c, "row": 2 * y + 1 - core}

    def own(g, source):
        k = lax.rem(g, K)
        lanes = pl.ds(pl.multiple_of(k * W, 128), W)
        return pltpu.make_async_copy(source.at[:, lanes], G.at[g, x, z], lsem.at[g])

    @pl.loop(0, K)
    def _(k):
        own(k, cs_ref).start()

    @pl.loop(0, K)
    def _(k):
        own(k + K, cf_ref).start()

    loads = [
        pltpu.make_async_copy(ds_ref, D.at[0], isem.at[0]),
        pltpu.make_async_copy(df_ref, D.at[1], isem.at[1]),
        pltpu.make_async_copy(e_ref, E, isem.at[2]),
        pltpu.make_async_copy(trail_ref, TR, isem.at[3]),
        pltpu.make_async_copy(rs_ref, R.at[:NB], isem.at[4]),
        pltpu.make_async_copy(rf_ref, R.at[NB:], isem.at[5]),
        pltpu.make_async_copy(crs_ref, CR.at[0], isem.at[6]),
        pltpu.make_async_copy(crf_ref, CR.at[1], isem.at[7]),
        pltpu.make_async_copy(ct_ref, CT, isem.at[8]),
    ]
    for load in loads:
        load.start()

    barrier = pltpu.get_barrier_semaphore()
    for pair in to:
        for device in pair:
            pl.semaphore_signal(barrier, 1, device_id=device, device_id_type=MESH)
    pl.semaphore_signal(barrier, 1, device_id=other, device_id_type=MESH)
    pl.semaphore_wait(barrier, 7)

    def hop(g, t, s, d, landing):
        i1, m1, p1 = ((x, x_m, x_p), (z, z_m, z_p))[t]
        i2, m2, p2 = ((z, z_m, z_p), (x, x_m, x_p))[t]
        near = lambda mine, minus, plus: (minus if d == 0 else plus)
        opposite = lambda mine: lax.rem(mine + 2, 4)
        rows, half = pl.ds(16 * t, 16), pl.ds(16 * t + 8 * d, 8)
        every = slice(None)
        if s == 0:
            a, b, part = (near(i1, m1, p1) if landing else i1), i2, rows
        elif s == 1:
            a, b, part = (opposite(i1) if landing else near(i1, m1, p1)), i2, half
        elif s == 2:
            a, b, part = every, (near(i2, m2, p2) if landing else i2), rows
        else:
            a, b, part = every, (opposite(i2) if landing else near(i2, m2, p2)), half
        ref = G.at[g, a, b, part] if t == 0 else G.at[g, b, a, part]
        axis = t if s < 2 else 1 - t
        index = t * 8 + s * 2 + d
        return pltpu.make_async_remote_copy(
            ref, ref, ssem.at[g, index], rsem.at[g, index], device_id=to[axis][d], device_id_type=MESH
        )

    def stage(g, s):
        if s == 0:
            own(g, cs_ref).wait()
        else:
            for t in range(2):
                for d in range(2):
                    hop(g, t, s - 1, d, True).wait_recv()
        if s < 4:
            for t in range(2):
                for d in range(2):
                    hop(g, t, s, d, False).start()

    def communicate(n):
        for s in (3, 2, 1, 0, 4):
            g = n + LEAD[s]

            @pl.when(g < N)
            def _():
                stage(g, s)

    def invert(panel):
        loads[panel].wait()
        blocks = [D[panel, HALF * i : HALF * i + HALF, HALF * i : HALF * i + HALF] for i in range(2)]
        for i, inverse in enumerate(invert_lower(blocks)):
            high, low = split(inverse.T)
            inv_s[2 * panel + i, :HALF] = high
            inv_s[2 * panel + i, HALF:] = low
        high, low = split(D[panel, HALF:, :HALF].T)
        off_s[panel, :HALF] = high
        off_s[panel, HALF:] = low

    def transpose_sub():
        loads[2].wait()
        high, low = split(E[...].T)
        e_s[:NB] = high
        e_s[NB:] = low
        acc[...] = jnp.zeros_like(acc)

    pieces = {1: functools.partial(invert, 0), 2: functools.partial(invert, 1), 3: transpose_sub}
    for i, hops in enumerate(FILL):
        for g, s in hops:
            stage(g, s)
        if i in pieces:
            pieces[i]()
    for load in loads[3:]:
        load.wait()

    def solve(right, panel):
        x1 = dot_tall(inv_s[2 * panel + 1], split(right[HALF:]))
        x1_parts = split(x1)
        left = right[:HALF] - dot_tall(off_s[panel], x1_parts)
        x0 = dot_tall(inv_s[2 * panel], split(left))
        return x0, x1, split(x0), x1_parts

    def put(k, panel, solved, out_ref):
        x0, x1, (h0, _), (h1, _) = solved
        lanes = pl.ds(pl.multiple_of(k * W, 128), W)
        for i in range(16):

            @pl.when(c == i)
            def _():
                out_ref[:, lanes] = (x0, x1)[i // 8][32 * (i % 8) : 32 * (i % 8) + 32]

        L[:HALF] = h0
        L[HALF:] = h1
        rows = TR[pl.ds(pl.multiple_of(k * W, 128), W)]
        for q in range(2):
            acc[panel, 2 * q : 2 * q + 2] += dot((h0, h1)[q], rows).reshape(2, 2, 64, rows.shape[1])

    far = lax.rem(y + 2, 4)

    def reduce_copies(panel, first, last):
        part = lambda buffer, i, rows: buffer.at[panel, i, rows]
        top, low, to_p, to_m = pl.ds(0, 32), pl.ds(32, 32), to[2][0], to[2][1]
        moves = [(acc.at[panel, q, 1 - core], XB.at[panel, q], other) for q in (far, y_p, y_m, y)] + [
            (part(PB, far, top), HB.at[panel, 0], to_p),
            (part(PB, far, low), HB.at[panel, 1], to_m),
            (part(PB, y_p, low), part(FB, 0, low), to_p),
            (part(PB, y_m, top), part(FB, 1, top), to_m),
            (part(PB, y_p, top), part(FB, 0, top), to_p),
            (part(PB, y_m, low), part(FB, 1, low), to_m),
        ]
        return [
            pltpu.make_async_remote_copy(
                src, dst, rs_send.at[panel, i], rs_recv.at[panel, i], device_id=device, device_id_type=MESH
            )
            for i, (src, dst, device) in list(enumerate(moves))[first:last]
        ]

    def start(panel, first, last):
        for copy in reduce_copies(panel, first, last):
            copy.start()

    def arrive(panel, first, last):
        for copy in reduce_copies(panel, first, last):
            copy.wait_recv()

    def reduce_step(panel, s, out_ref):
        if s == 0:
            start(panel, 0, 4)
        elif s == 1:
            for i, q in enumerate((far, y_p, y_m, y)):
                arrive(panel, i, i + 1)
                PB[panel, q] = acc[panel, q, core] + XB[panel, q]
                if i == 0:
                    start(panel, 4, 6)
                elif i < 3:
                    start(panel, 5 + i, 6 + i)
        elif s == 2:
            arrive(panel, 4, 6)
            PB[panel, y_p, :32] += HB[panel, 0]
            PB[panel, y_m, 32:] += HB[panel, 1]
            start(panel, 8, 10)
        else:
            arrive(panel, 6, 10)
            out_ref[...] = CR[panel] - ((PB[panel, y] + FB[panel, 0]) + FB[panel, 1])

    def trail(k, panel):
        rows = pl.ds(pl.multiple_of(k * W, W), W)
        right = R[NB * panel : NB * panel + NB]
        update = lax.dot_general(L[...], right, (((0,), (0,)), ((), ())), preferred_element_type=F32)
        CT[rows] -= update

    @pl.loop(0, K)
    def _(k):
        communicate(k)
        solved = solve(G[k].reshape(NB, W), 0)
        put(k, 0, solved, ss_ref)
        trail(k, 0)
        T[k] = dot_tall(e_s[...], tuple(jnp.concatenate(p, axis=0) for p in zip(solved[2], solved[3])))

    @pl.loop(0, K)
    def _(k):
        communicate(K + k)
        for s in range(4):

            @pl.when(k == s)
            def _():
                reduce_step(0, s, nrs_ref)

        @pl.when(k >= 1)
        def _():
            trail(k - 1, 1)

        put(k, 1, solve(G[K + k].reshape(NB, W) - T[k], 1), sf_ref)

    reduce_step(1, 0, nrf_ref)
    trail(K - 1, 1)
    reduce_step(1, 1, nrf_ref)

    @pl.loop(0, N)
    def _(g):
        for s in range(4):
            for t in range(2):
                for d in range(2):
                    hop(g, t, s, d, False).wait_send()

    reduce_step(1, 2, nrf_ref)

    reduce_step(1, 3, nrf_ref)
    for panel in range(2):
        for copy in reduce_copies(panel, 0, 10):
            copy.wait_send()


def on_device(
    trail_rows, rows_first, rows_second, diag_first, diag_second, sub_block,
    cot_first, cot_second, cot_trail, cot_rows_first, cot_rows_second,
):
    rows, cols = trail_rows.shape
    K = rows // W
    shape = jax.ShapeDtypeStruct
    hbm = pl.BlockSpec(memory_space=pl.ANY)
    vmem = pl.BlockSpec(memory_space=pltpu.VMEM)
    dma = pltpu.SemaphoreType.DMA
    results = pl.pallas_call(
        kernel,
        out_shape=(
            pltpu.VMEM((rows, cols), F32),
            pltpu.VMEM((64, cols), F32),
            pltpu.VMEM((64, cols), F32),
            pltpu.VMEM((32, rows), F32),
            pltpu.VMEM((32, rows), F32),
        ),
        in_specs=[hbm] * 11,
        out_specs=(vmem,) * 5,
        scratch_shapes=[
            pltpu.VMEM((2 * K, 4, 4, 32, W), F32),
            pltpu.VMEM((K, NB, W), F32),
            pltpu.VMEM((NB, W), BF),
            pltpu.VMEM((rows, cols), BF),
            pltpu.VMEM((2 * NB, cols), BF),
            pltpu.VMEM((2, NB, NB), F32),
            pltpu.VMEM((NB, NB), F32),
            pltpu.VMEM((2, 4, 2, 64, cols), F32),
            pltpu.VMEM((2, 4, 64, cols), F32),
            pltpu.VMEM((2, 4, 64, cols), F32),
            pltpu.VMEM((2, 2, 32, cols), F32),
            pltpu.VMEM((2, 2, 64, cols), F32),
            pltpu.VMEM((2, 64, cols), F32),
            pltpu.VMEM((4, NB, HALF), BF),
            pltpu.VMEM((2, NB, HALF), BF),
            pltpu.VMEM((2 * NB, NB), BF),
            dma((2 * K,)),
            dma((9,)),
            dma((2 * K, 16)),
            dma((2 * K, 16)),
            dma((2, 10)),
            dma((2, 10)),
        ],
        compiler_params=pltpu.CompilerParams(
            collective_id=0, has_side_effects=True, vmem_limit_bytes=50 * 1024 * 1024
        ),
    )(
        cot_second.T, cot_first.T, trail_rows, rows_second, rows_first, diag_second, diag_first,
        sub_block, cot_trail, cot_rows_first, cot_rows_second,
    )
    new_trail, new_first, new_second, first_t, second_t = results
    return new_trail, new_first, new_second, first_t.T, second_t.T


def solution(mesh):
    both = P("row", "col")
    col = P(None, "col")
    return jax.shard_map(
        on_device,
        mesh=mesh,
        in_specs=(both, col, col, P(), P(), P(), both, both, both, both, both),
        out_specs=(both,) * 5,
        check_vma=False,
    )
```

time: 109 us -> 98.1 us (0.90)
  Pallas kernels: 98 us -> 91.1 us
  local copies, waits for them, and re-layouts: 9.1 us -> 5.51 us
    pallas_call x1, Pallas kernels: 98 us -> 91.1 us  [on_device(): pl.pallas_call(kernel, out_shape=(pltpu.VMEM((rows, cols), F32), pltpu.VM...]
    unnamed x13 -> x5, local copies, waits for them, and re-layouts: 9.1 us -> 5.51 us
where the time goes in v2:
time: 98.1 us; the launch traced here: 97.2 us
  Pallas kernels  91.1 us (93%)
  local copies, waits for them, and re-layouts  5.51 us (6%)
    pallas_call x1, Pallas kernels, on_device(): pl.pallas_call(kernel, out_shape=(pltpu.VMEM((rows, cols), F32), pltpu.VM...  91.1 us
    unnamed x5, local copies, waits for them, and re-layouts  5.51 us

profile of v2, /device:TPU:0, one launch (start us, length us, event | category | flops | bytes accessed | tf_op | source)
XLA Modules:
  0.0 97.2 jit_solution(184917377331846617)
XLA Ops:
  0.6 91.1 %shard_map.146 = (f32[3072,512]{1,0:T(8,128)S(1)}, f32[64,512]{1,0:T(8,128)S(1)}, f32[64,512]{1,0:T(8,128)S(1)}, f32[32,3072]{1,0:T(8,128)S(1)}, f32[32,3072]{1,0:T(8,128)S(1)}) custom-call(f32[32,3072]{1,0:T(8,128)} %bitcast.6, f32[32,3072]{1,0:T(8,128)} %bitcast.7, bf16[3072,512]{1,0:T(8,128)(2,1)} %trail_ref.1, bf16[512,512]{1,0:T(8,128)(2,1)} %rs_ref.1, ...), custom_call_target="tpu_custom_call" | custom-call | tf_op jit(solution)/shard_map/pallas_call | solution.py:350
  91.7 2.7 %copy.21 = f32[3072,512]{1,0:T(8,128)} copy(f32[3072,512]{1,0:T(8,128)S(1)} %get-tuple-element.15) | data formatting | bytes 12582912
  94.4 0.7 copy.22
  95.1 0.7 copy.23
  95.7 0.7 copy.24
  96.5 0.7 copy.25

commit v3 on v2

--- a/solution.py
+++ b/solution.py
@@ -96,11 +96,12 @@
 
 def kernel(
     cs_ref, cf_ref, trail_ref, rs_ref, rf_ref, ds_ref, df_ref, e_ref, ct_ref, crf_ref, crs_ref,
-    CT, nrf_ref, nrs_ref, sf_ref, ss_ref,
+    CT, n_ref, s_ref,
     G, T, L, TR, R, D, E, acc, XB, PB, HB, FB, CR, inv_s, off_s, e_s,
     lsem, isem, ssem, rsem, rs_send, rs_recv,
 ):
     K = G.shape[0] // 2
+    nrf_ref, nrs_ref, sf_ref, ss_ref = n_ref.at[0], n_ref.at[1], s_ref.at[0], s_ref.at[1]
     N = 2 * K
     c = lax.axis_index("col")
     r = lax.axis_index("row")
@@ -184,8 +185,8 @@
                 for d in range(2):
                     hop(g, t, s, d, False).start()
 
-    def communicate(n):
-        for s in (3, 2, 1, 0, 4):
+    def communicate(n, hops):
+        for s in hops:
             g = n + LEAD[s]
 
             @pl.when(g < N)
@@ -219,15 +220,23 @@
     for load in loads[3:]:
         load.wait()
 
-    def solve(right, panel):
-        x1 = dot_tall(inv_s[2 * panel + 1], split(right[HALF:]))
-        x1_parts = split(x1)
-        left = right[:HALF] - dot_tall(off_s[panel], x1_parts)
-        x0 = dot_tall(inv_s[2 * panel], split(left))
-        return x0, x1, split(x0), x1_parts
-
-    def put(k, panel, solved, out_ref):
-        x0, x1, (h0, _), (h1, _) = solved
+    def solve_part(right, panel, q):
+        x = dot_tall(inv_s[2 * panel + q], split(right))
+        return x, split(x)
+
+    def add_product(k, panel, q, high):
+        rows = TR[pl.ds(pl.multiple_of(k * W, 128), W)]
+        acc[panel, 2 * q : 2 * q + 2] += dot(high, rows).reshape(2, 2, 64, rows.shape[1])
+
+    def chunk(k, panel, right, out_ref, after=lambda q: None):
+        x1, parts1 = solve_part(right[HALF:], panel, 1)
+        L[HALF:] = parts1[0]
+        add_product(k, panel, 1, parts1[0])
+        after(1)
+        x0, parts0 = solve_part(right[:HALF] - dot_tall(off_s[panel], parts1), panel, 0)
+        L[:HALF] = parts0[0]
+        add_product(k, panel, 0, parts0[0])
+        after(0)
         lanes = pl.ds(pl.multiple_of(k * W, 128), W)
         for i in range(16):
 
@@ -235,18 +244,14 @@
             def _():
                 out_ref[:, lanes] = (x0, x1)[i // 8][32 * (i % 8) : 32 * (i % 8) + 32]
 
-        L[:HALF] = h0
-        L[HALF:] = h1
-        rows = TR[pl.ds(pl.multiple_of(k * W, 128), W)]
-        for q in range(2):
-            acc[panel, 2 * q : 2 * q + 2] += dot((h0, h1)[q], rows).reshape(2, 2, 64, rows.shape[1])
+        return parts0, parts1
 
     far = lax.rem(y + 2, 4)
 
     def reduce_copies(panel, first, last):
         part = lambda buffer, i, rows: buffer.at[panel, i, rows]
         top, low, to_p, to_m = pl.ds(0, 32), pl.ds(32, 32), to[2][0], to[2][1]
-        moves = [(acc.at[panel, q, 1 - core], XB.at[panel, q], other) for q in (far, y_p, y_m, y)] + [
+        moves = [(acc.at[panel, q, 1 - core], XB.at[panel, q], other) for q in range(4)] + [
             (part(PB, far, top), HB.at[panel, 0], to_p),
             (part(PB, far, low), HB.at[panel, 1], to_m),
             (part(PB, y_p, low), part(FB, 0, low), to_p),
@@ -274,7 +279,10 @@
             start(panel, 0, 4)
         elif s == 1:
             for i, q in enumerate((far, y_p, y_m, y)):
-                arrive(panel, i, i + 1)
+                pltpu.make_async_remote_copy(
+                    acc.at[panel, q, 1 - core], XB.at[panel, q], rs_send.at[panel, q], rs_recv.at[panel, q],
+                    device_id=other, device_id_type=MESH,
+                ).wait_recv()
                 PB[panel, q] = acc[panel, q, core] + XB[panel, q]
                 if i == 0:
                     start(panel, 4, 6)
@@ -297,15 +305,14 @@
 
     @pl.loop(0, K)
     def _(k):
-        communicate(k)
-        solved = solve(G[k].reshape(NB, W), 0)
-        put(k, 0, solved, ss_ref)
+        communicate(k, (3, 2, 1, 0, 4))
+        parts = chunk(k, 0, G[k].reshape(NB, W), ss_ref)
         trail(k, 0)
-        T[k] = dot_tall(e_s[...], tuple(jnp.concatenate(p, axis=0) for p in zip(solved[2], solved[3])))
-
-    @pl.loop(0, K)
+        T[k] = dot_tall(e_s[...], tuple(jnp.concatenate(p, axis=0) for p in zip(*parts)))
+
+    @pl.loop(0, K - 1)
     def _(k):
-        communicate(K + k)
+        communicate(K + k, (3, 2, 1, 0))
         for s in range(4):
 
             @pl.when(k == s)
@@ -316,9 +323,12 @@
         def _():
             trail(k - 1, 1)
 
-        put(k, 1, solve(G[K + k].reshape(NB, W) - T[k], 1), sf_ref)
-
-    reduce_step(1, 0, nrf_ref)
+        communicate(K + k, (4,))
+        chunk(k, 1, G[K + k].reshape(NB, W) - T[k], sf_ref)
+
+    trail(K - 2, 1)
+    stage(N - 1, 4)
+    chunk(K - 1, 1, G[N - 1].reshape(NB, W) - T[K - 1], sf_ref, lambda q: start(1, 2 * q, 2 * q + 2))
     trail(K - 1, 1)
     reduce_step(1, 1, nrf_ref)
 
@@ -351,13 +361,11 @@
         kernel,
         out_shape=(
             pltpu.VMEM((rows, cols), F32),
-            pltpu.VMEM((64, cols), F32),
-            pltpu.VMEM((64, cols), F32),
-            pltpu.VMEM((32, rows), F32),
-            pltpu.VMEM((32, rows), F32),
+            pltpu.VMEM((2, 64, cols), F32),
+            pltpu.VMEM((2, 32, rows), F32),
         ),
         in_specs=[hbm] * 11,
-        out_specs=(vmem,) * 5,
+        out_specs=(vmem,) * 3,
         scratch_shapes=[
             pltpu.VMEM((2 * K, 4, 4, 32, W), F32),
             pltpu.VMEM((K, NB, W), F32),
@@ -389,7 +397,7 @@
         cot_second.T, cot_first.T, trail_rows, rows_second, rows_first, diag_second, diag_first,
         sub_block, cot_trail, cot_rows_first, cot_rows_second,
     )
-    new_trail, new_first, new_second, first_t, second_t = results
+    new_trail, (new_first, new_second), (first_t, second_t) = results[0], results[1], results[2]
     return new_trail, new_first, new_second, first_t.T, second_t.T
 
 

time: 98.1 us -> 95 us (0.968)
  Pallas kernels: 91.1 us -> 89.7 us
  local copies, waits for them, and re-layouts: 5.51 us -> 4.35 us
    unnamed x5 -> x1, local copies, waits for them, and re-layouts: 5.51 us -> 2.71 us
    pallas_call x1, Pallas kernels: 91.1 us -> 89.7 us  [on_device(): pl.pallas_call(kernel, out_shape=(pltpu.VMEM((rows, cols), F32), pltpu.VM...]
where the time goes in v3:
time: 95 us; the launch traced here: 94.7 us
  Pallas kernels  89.7 us (94%)
  local copies, waits for them, and re-layouts  4.35 us (5%)
    pallas_call x1, Pallas kernels, on_device(): pl.pallas_call(kernel, out_shape=(pltpu.VMEM((rows, cols), F32), pltpu.VM...  89.7 us
    unnamed x1, local copies, waits for them, and re-layouts  2.71 us

profile of v3, /device:TPU:0, one launch (start us, length us, event | category | flops | bytes accessed | tf_op | source)
XLA Modules:
  0.0 94.7 jit_solution(9393349256372031087)
XLA Ops:
  0.6 89.7 %shard_map.146 = (f32[3072,512]{1,0:T(8,128)S(1)}, f32[2,64,512]{2,1,0:T(8,128)S(1)}, f32[2,32,3072]{2,1,0:T(8,128)S(1)}) custom-call(f32[32,3072]{1,0:T(8,128)} %bitcast.14, f32[32,3072]{1,0:T(8,128)} %bitcast.15, bf16[3072,512]{1,0:T(8,128)(2,1)} %trail_ref.1, bf16[512,512]{1,0:T(8,128)(2,1)} %rs_ref.1, bf16[512,512]{1,0:T(8,128)(2,1)} %rf_ref.1, ...), custom_call_target="tpu_custom_call" | custom-call | tf_op jit(solution)/shard_map/pallas_call | solution.py:360
  90.3 2.7 %copy.17 = f32[3072,512]{1,0:T(8,128)} copy(f32[3072,512]{1,0:T(8,128)S(1)} %get-tuple-element.15) | data formatting | bytes 12582912
  93.0 0.7 slice_bitcast_fusion.2
  93.7 0.9 slice_bitcast_fusion

commit v4 on v3

--- a/solution.py
+++ b/solution.py
@@ -230,11 +230,12 @@
 
     def chunk(k, panel, right, out_ref, after=lambda q: None):
         x1, parts1 = solve_part(right[HALF:], panel, 1)
-        L[HALF:] = parts1[0]
+        slot = lax.rem(k, 3)
+        L[slot, HALF:] = parts1[0]
         add_product(k, panel, 1, parts1[0])
         after(1)
         x0, parts0 = solve_part(right[:HALF] - dot_tall(off_s[panel], parts1), panel, 0)
-        L[:HALF] = parts0[0]
+        L[slot, :HALF] = parts0[0]
         add_product(k, panel, 0, parts0[0])
         after(0)
         lanes = pl.ds(pl.multiple_of(k * W, 128), W)
@@ -300,7 +301,7 @@
     def trail(k, panel):
         rows = pl.ds(pl.multiple_of(k * W, W), W)
         right = R[NB * panel : NB * panel + NB]
-        update = lax.dot_general(L[...], right, (((0,), (0,)), ((), ())), preferred_element_type=F32)
+        update = lax.dot_general(L[lax.rem(k, 3)], right, (((0,), (0,)), ((), ())), preferred_element_type=F32)
         CT[rows] -= update
 
     @pl.loop(0, K)
@@ -319,18 +320,20 @@
             def _():
                 reduce_step(0, s, nrs_ref)
 
-        @pl.when(k >= 1)
+        @pl.when((k >= 1) & (k <= K - 3))
         def _():
             trail(k - 1, 1)
 
         communicate(K + k, (4,))
         chunk(k, 1, G[K + k].reshape(NB, W) - T[k], sf_ref)
 
-    trail(K - 2, 1)
     stage(N - 1, 4)
     chunk(K - 1, 1, G[N - 1].reshape(NB, W) - T[K - 1], sf_ref, lambda q: start(1, 2 * q, 2 * q + 2))
+    trail(K - 3, 1)
+    reduce_step(1, 1, nrf_ref)
+    trail(K - 2, 1)
+    reduce_step(1, 2, nrf_ref)
     trail(K - 1, 1)
-    reduce_step(1, 1, nrf_ref)
 
     @pl.loop(0, N)
     def _(g):
@@ -338,8 +341,6 @@
             for t in range(2):
                 for d in range(2):
                     hop(g, t, s, d, False).wait_send()
-
-    reduce_step(1, 2, nrf_ref)
 
     reduce_step(1, 3, nrf_ref)
     for panel in range(2):
@@ -369,7 +370,7 @@
         scratch_shapes=[
             pltpu.VMEM((2 * K, 4, 4, 32, W), F32),
             pltpu.VMEM((K, NB, W), F32),
-            pltpu.VMEM((NB, W), BF),
+            pltpu.VMEM((3, NB, W), BF),
             pltpu.VMEM((rows, cols), BF),
             pltpu.VMEM((2 * NB, cols), BF),
             pltpu.VMEM((2, NB, NB), F32),

time: 95 us -> 95.4 us (level)
  no operation moved by 1% of the time
where the time goes in v4:
time: 95.4 us; the launch traced here: 94.7 us
  Pallas kernels  89.7 us (94%)
  local copies, waits for them, and re-layouts  4.35 us (5%)
    pallas_call x1, Pallas kernels, on_device(): pl.pallas_call(kernel, out_shape=(pltpu.VMEM((rows, cols), F32), pltpu.VM...  89.7 us
    unnamed x1, local copies, waits for them, and re-layouts  2.71 us

profile of v4, /device:TPU:0, one launch (start us, length us, event | category | flops | bytes accessed | tf_op | source)
XLA Modules:
  0.0 94.7 jit_solution(6774048011239079457)
XLA Ops:
  0.6 89.7 %shard_map.146 = (f32[3072,512]{1,0:T(8,128)S(1)}, f32[2,64,512]{2,1,0:T(8,128)S(1)}, f32[2,32,3072]{2,1,0:T(8,128)S(1)}) custom-call(f32[32,3072]{1,0:T(8,128)} %bitcast.14, f32[32,3072]{1,0:T(8,128)} %bitcast.15, bf16[3072,512]{1,0:T(8,128)(2,1)} %trail_ref.1, bf16[512,512]{1,0:T(8,128)(2,1)} %rs_ref.1, bf16[512,512]{1,0:T(8,128)(2,1)} %rf_ref.1, ...), custom_call_target="tpu_custom_call" | custom-call | tf_op jit(solution)/shard_map/pallas_call | solution.py:361
  90.3 2.7 %copy.17 = f32[3072,512]{1,0:T(8,128)} copy(f32[3072,512]{1,0:T(8,128)S(1)} %get-tuple-element.15) | data formatting | bytes 12582912
  93.0 0.7 slice_bitcast_fusion.2
  93.7 0.9 slice_bitcast_fusion
